TPU v7x, 32 devices: a whole 2x2x4 slice. The times are simulated.
32 devices in a mesh: seq: 16 (over z, x, core), dp: 2 (over y).
Axes of the slice: x: 2, y: 2, z: 4, core: 2. Of those that a mesh axis runs over, the one named last changes fastest.
Arguments:
- queries: bfloat16 [2, 1024, 2048], P(None, 'seq', 'dp'), may hold values from -10 to 10
- key_rows: bfloat16 [2, 1024, 2048], P(None, 'seq', 'dp'), may hold values from -10 to 10
- value_rows: bfloat16 [2, 1024, 2048], P(None, 'seq', 'dp'), may hold values from -6 to 6
- query_tangent: bfloat16 [2, 1024, 2048], P(None, 'seq', 'dp'), may hold values from -6 to 6
- key_tangent: bfloat16 [2, 1024, 2048], P(None, 'seq', 'dp'), may hold values from -6 to 6
- out_adjoint: bfloat16 [2, 1024, 2048], P(None, 'seq', 'dp'), may hold values from -6 to 6
Outputs:
- query_product: bfloat16 [2, 1024, 2048], P(None, 'seq', 'dp')
- key_product: bfloat16 [2, 1024, 2048], P(None, 'seq', 'dp')
- value_product: bfloat16 [2, 1024, 2048], P(None, 'seq', 'dp')
- curvature: float32 [2, 16], replicated
All inputs are finite; a program needn't handle non-finite values.
Results may differ from a plain program's by a relative error of at most 0.0051.
Values may be sent and summed in bfloat16 or wider, within the bound.
A program may use at most 64 MiB of HBM per device.

v0:
```python
import jax
import jax.numpy as jnp
from jax import lax
from jax.sharding import PartitionSpec as P

HEAD_DIM = 128


def inner_rows(left, right):
    return lax.dot_general(
        left, right, (((1,), (1,)), ((), ())), preferred_element_type=jnp.float32
    )


def inner_cols(left, right):
    return lax.dot_general(
        left, right, (((0,), (0,)), ((), ())), preferred_element_type=jnp.float32
    )


def score_block(query, keyset, tquery, tkey, start, block_size):
    factor = HEAD_DIM ** (-0.5)
    stop = start + block_size
    query_block = query[start:stop]
    key_block = keyset[:stop]
    scores = factor * inner_rows(query_block, key_block)
    row_index = start + jnp.arange(block_size)[:, None]
    col_index = jnp.arange(stop)[None, :]
    scores = jnp.where(row_index >= col_index, scores, -jnp.inf)
    top_score = jnp.max(scores, axis=1, keepdims=True)
    weights = jnp.exp(scores - top_score)
    probs = weights / jnp.sum(weights, axis=1, keepdims=True)
    tangent_scores = factor * (
        inner_rows(tquery[start:stop], key_block) + inner_rows(query_block, tkey[:stop])
    )
    mean_tangent = jnp.sum(probs * tangent_scores, axis=1, keepdims=True)
    tangent_probs = probs * (tangent_scores - mean_tangent)
    return (probs, tangent_probs)


def head_work(tensors):
    query, keyset, values_in, tquery, tkey, adjoint = tensors
    factor = HEAD_DIM ** (-0.5)
    length = query.shape[0]
    block_size = min(512, length)
    key_hvp = jnp.zeros((length, HEAD_DIM), jnp.float32)
    value_hvp = jnp.zeros((length, HEAD_DIM), jnp.float32)
    query_parts = []
    for number in range(length // block_size):
        start = number * block_size
        stop = start + block_size
        probs, tangent_probs = score_block(query, keyset, tquery, tkey, start, block_size)
        adj_block = adjoint[start:stop]
        grad_probs = inner_rows(adj_block, values_in[:stop])
        delta = jnp.sum(probs * grad_probs, axis=1, keepdims=True)
        centered = grad_probs - delta
        grad_scores = probs * centered
        tangent_delta = jnp.sum(tangent_probs * grad_probs, axis=1, keepdims=True)
        second_scores = tangent_probs * centered - probs * tangent_delta
        tprob_low = tangent_probs.astype(jnp.bfloat16)
        gscore_low = grad_scores.astype(jnp.bfloat16)
        second_low = second_scores.astype(jnp.bfloat16)
        value_hvp = value_hvp.at[:stop].add(inner_cols(tprob_low, adj_block))
        query_parts.append(
            factor
            * (
                jnp.dot(second_low, keyset[:stop], preferred_element_type=jnp.float32)
                + jnp.dot(gscore_low, tkey[:stop], preferred_element_type=jnp.float32)
            )
        )
        key_hvp = key_hvp.at[:stop].add(
            factor
            * (
                inner_cols(second_low, query[start:stop])
                + inner_cols(gscore_low, tquery[start:stop])
            )
        )
    query_hvp = jnp.concatenate(query_parts, axis=0)
    kappa = jnp.sum(tquery.astype(jnp.float32) * query_hvp) + jnp.sum(
        tkey.astype(jnp.float32) * key_hvp
    )
    return (query_hvp, key_hvp, value_hvp, kappa)


def local(queries, key_rows, value_rows, query_tangent, key_tangent, out_adjoint):
    batch_count = queries.shape[0]
    tokens_here = queries.shape[1]
    local_heads = queries.shape[2] // HEAD_DIM

    def to_items(tensor):
        shaped = tensor.reshape(batch_count, tokens_here, local_heads, HEAD_DIM)
        return jnp.transpose(shaped, (0, 2, 1, 3)).reshape(
            batch_count * local_heads, tokens_here, HEAD_DIM
        )

    parts = (
        lax.all_to_all(to_items(queries), "seq", split_axis=0, concat_axis=1, tiled=True),
        lax.all_to_all(to_items(key_rows), "seq", split_axis=0, concat_axis=1, tiled=True),
        lax.all_to_all(to_items(value_rows), "seq", split_axis=0, concat_axis=1, tiled=True),
        lax.all_to_all(to_items(query_tangent), "seq", split_axis=0, concat_axis=1, tiled=True),
        lax.all_to_all(to_items(key_tangent), "seq", split_axis=0, concat_axis=1, tiled=True),
        lax.all_to_all(to_items(out_adjoint), "seq", split_axis=0, concat_axis=1, tiled=True),
    )
    item_count = parts[0].shape[0]
    item = 0
    tensors = tuple((part[item] for part in parts))
    query_hvp, key_hvp, value_hvp, kappa = head_work(tensors)
    query_items = [query_hvp.astype(jnp.bfloat16)]
    key_items = [key_hvp.astype(jnp.bfloat16)]
    value_items = [value_hvp.astype(jnp.bfloat16)]
    kappas = [kappa]
    returned = (
        lax.all_to_all(jnp.stack(query_items), "seq", split_axis=1, concat_axis=0, tiled=True),
        lax.all_to_all(jnp.stack(key_items), "seq", split_axis=1, concat_axis=0, tiled=True),
        lax.all_to_all(jnp.stack(value_items), "seq", split_axis=1, concat_axis=0, tiled=True),
    )

    def to_tokens(tensor):
        shaped = tensor.reshape(batch_count, local_heads, tokens_here, HEAD_DIM)
        return jnp.transpose(shaped, (0, 2, 1, 3)).reshape(
            batch_count, tokens_here, local_heads * HEAD_DIM
        )

    outputs = tuple((to_tokens(piece) for piece in returned))
    heads_total = local_heads * lax.axis_size("dp")
    batch_index = jnp.arange(batch_count)[:, None]
    head_index = jnp.arange(heads_total)[None, :]
    item = 0
    global_item = lax.axis_index("seq") * item_count + item
    batch_here = global_item // local_heads
    head_here = lax.axis_index("dp") * local_heads + global_item % local_heads
    hit = jnp.logical_and(batch_index == batch_here, head_index == head_here)
    board = jnp.where(hit, kappas[item], 0.0)
    curvature = lax.psum(board, ("seq", "dp"))
    return (outputs[0], outputs[1], outputs[2], curvature)


def solution(mesh):
    return jax.shard_map(
        local,
        mesh=mesh,
        in_specs=(
            P(None, "seq", "dp"),
            P(None, "seq", "dp"),
            P(None, "seq", "dp"),
            P(None, "seq", "dp"),
            P(None, "seq", "dp"),
            P(None, "seq", "dp"),
        ),
        out_specs=(P(None, "seq", "dp"), P(None, "seq", "dp"), P(None, "seq", "dp"), P()),
        check_vma=False,
    )
```

profile of v0, /device:TPU:0, one launch (start us, length us, event | category | flops | bytes accessed | tf_op | source)
XLA Modules:
  0.0 181.6 jit_solution(2033972565623164572)
XLA Ops:
  2.5 7.4 %all-to-all-start = ((bf16[16,64,128]{2,1,0:T(8,128)(2,1)}), bf16[16,64,128]{2,1,0:T(8,128)(2,1)S(1)}, u32[]{:S(2)}, u32[]{:S(2)}) async-start(bf16[16,64,128]{2,1,0:T(8,128)(2,1)} %bitcast.1), calls=%async_computation | async-start | bytes 524288 | tf_op jit(solution)/shard_map/all_to_all | solution.py:97
  10.9 9.0 %all-to-all-done = bf16[16,64,128]{2,1,0:T(8,128)(2,1)S(1)} async-done(((bf16[16,64,128]{2,1,0:T(8,128)(2,1)}), bf16[16,64,128]{2,1,0:T(8,128)(2,1)S(1)}, u32[]{:S(2)}, u32[]{:S(2)}) %all-to-all-start) | async-done | bytes 262176 | tf_op jit(solution)/shard_map/all_to_all | solution.py:97
  19.9 3.5 %all-to-all-start.1 = ((bf16[16,64,128]{2,1,0:T(8,128)(2,1)}), bf16[16,64,128]{2,1,0:T(8,128)(2,1)S(1)}, u32[]{:S(2)}, u32[]{:S(2)}) async-start(bf16[16,64,128]{2,1,0:T(8,128)(2,1)} %bitcast.4), calls=%async_computation.1 | async-start | bytes 524288 | tf_op jit(solution)/shard_map/all_to_all | solution.py:98
  24.4 9.0 %all-to-all-done.1 = bf16[16,64,128]{2,1,0:T(8,128)(2,1)S(1)} async-done(((bf16[16,64,128]{2,1,0:T(8,128)(2,1)}), bf16[16,64,128]{2,1,0:T(8,128)(2,1)S(1)}, u32[]{:S(2)}, u32[]{:S(2)}) %all-to-all-start.1) | async-done | bytes 262176 | tf_op jit(solution)/shard_map/all_to_all | solution.py:98
  33.4 3.5 %all-to-all-start.2 = ((bf16[16,64,128]{2,1,0:T(8,128)(2,1)}), bf16[16,64,128]{2,1,0:T(8,128)(2,1)S(1)}, u32[]{:S(2)}, u32[]{:S(2)}) async-start(bf16[16,64,128]{2,1,0:T(8,128)(2,1)} %bitcast.7), calls=%async_computation.2 | async-start | bytes 524288 | tf_op jit(solution)/shard_map/all_to_all | solution.py:100
  40.5 6.5 %all-to-all-done.2 = bf16[16,64,128]{2,1,0:T(8,128)(2,1)S(1)} async-done(((bf16[16,64,128]{2,1,0:T(8,128)(2,1)}), bf16[16,64,128]{2,1,0:T(8,128)(2,1)S(1)}, u32[]{:S(2)}, u32[]{:S(2)}) %all-to-all-start.2) | async-done | bytes 262176 | tf_op jit(solution)/shard_map/all_to_all | solution.py:100
  47.0 3.5 %all-to-all-start.4 = ((bf16[16,64,128]{2,1,0:T(8,128)(2,1)}), bf16[16,64,128]{2,1,0:T(8,128)(2,1)S(1)}, u32[]{:S(2)}, u32[]{:S(2)}) async-start(bf16[16,64,128]{2,1,0:T(8,128)(2,1)} %bitcast.13), calls=%async_computation.4 | async-start | bytes 524288 | tf_op jit(solution)/shard_map/all_to_all | solution.py:102
  51.8 1.8 fusion.25
  53.6 6.9 %all-to-all-done.4 = bf16[16,64,128]{2,1,0:T(8,128)(2,1)S(1)} async-done(((bf16[16,64,128]{2,1,0:T(8,128)(2,1)}), bf16[16,64,128]{2,1,0:T(8,128)(2,1)S(1)}, u32[]{:S(2)}, u32[]{:S(2)}) %all-to-all-start.4) | async-done | bytes 262176 | tf_op jit(solution)/shard_map/all_to_all | solution.py:102
  60.5 3.5 %all-to-all-start.3 = ((bf16[16,64,128]{2,1,0:T(8,128)(2,1)}), bf16[16,64,128]{2,1,0:T(8,128)(2,1)S(1)}, u32[]{:S(2)}, u32[]{:S(2)}) async-start(bf16[16,64,128]{2,1,0:T(8,128)(2,1)} %bitcast.10), calls=%async_computation.3 | async-start | bytes 524288 | tf_op jit(solution)/shard_map/all_to_all | solution.py:101
  65.3 8.7 %all-to-all-done.3 = bf16[16,64,128]{2,1,0:T(8,128)(2,1)S(1)} async-done(((bf16[16,64,128]{2,1,0:T(8,128)(2,1)}), bf16[16,64,128]{2,1,0:T(8,128)(2,1)S(1)}, u32[]{:S(2)}, u32[]{:S(2)}) %all-to-all-start.3) | async-done | bytes 262176 | tf_op jit(solution)/shard_map/all_to_all | solution.py:101
  74.0 3.7 %all-to-all-start.5 = ((bf16[16,64,128]{2,1,0:T(8,128)(2,1)}), bf16[16,64,128]{2,1,0:T(8,128)(2,1)S(1)}, u32[]{:S(2)}, u32[]{:S(2)}) async-start(bf16[16,64,128]{2,1,0:T(8,128)(2,1)} %bitcast.16), calls=%async_computation.5 | async-start | bytes 524288 | tf_op jit(solution)/shard_map/all_to_all | solution.py:99
  79.3 2.1 %multiply_reduce_fusion.2 = (f32[512]{0:T(512)S(1)}, f32[512,1024]{1,0:T(8,128)}) fusion(f32[512]{0:T(512)S(1)} %fusion.1, f32[512,1024]{1,0:T(8,128)S(1)} %get-tuple-element.85, f32[512]{0:T(512)S(1)} %get-tuple-element.84, f32[512,1024]{1,0:T(8,128)S(1)} %copy-done.8, bf16[512,128]{1,0:T(8,128)(2,1)S(1)} %bitcast.176, bf16[1024,128]{1,0:T(8,128)(2,1)S(1)} %bitcast.144), kind=kOutput, calls=%fused_computation.5 | convolution fusion | flops 137362944 | bytes 6690816 | tf_op jit(solution)/shard_map/dot_general | solution.py:10
  81.4 6.1 %all-to-all-done.5 = bf16[16,64,128]{2,1,0:T(8,128)(2,1)S(1)} async-done(((bf16[16,64,128]{2,1,0:T(8,128)(2,1)}), bf16[16,64,128]{2,1,0:T(8,128)(2,1)S(1)}, u32[]{:S(2)}, u32[]{:S(2)}) %all-to-all-start.5) | async-done | bytes 262176 | tf_op jit(solution)/shard_map/all_to_all | solution.py:99
  87.5 2.7 %multiply_reduce_fusion.1 = (f32[512]{0:T(512)S(1)}, f32[512]{0:T(512)S(1)}, f32[512,1024]{1,0:T(8,128)S(1)}) fusion(f32[512]{0:T(512)S(1)} %fusion.1, f32[512,1024]{1,0:T(8,128)S(1)} %get-tuple-element.85, f32[512]{0:T(512)S(1)} %get-tuple-element.84, f32[512,1024]{1,0:T(8,128)} %get-tuple-element.87, f32[512]{0:T(512)S(1)} %get-tuple-element.86, ...), kind=kOutput, calls=%fused_computation.3 | convolution fusion | flops 138411008 | bytes 6694912 | tf_op jit(solution)/shard_map/dot_general | solution.py:10
  90.3 1.2 multiply_convert_fusion
  91.6 1.1 fusion.26
  92.7 1.3 fusion.28
  97.3 1.3 multiply_convert_fusion.1
  99.7 1.2 fusion.9
  101.8 2.2 %reduce.12 = bf16[1024,128]{1,0:T(8,128)(2,1)S(1)} reduce(bf16[1024,1,128]{2,1,0:T(2,128)(2,1)S(1)} %bitcast.149, bf16[]{:T(256)} %broadcast.116), dimensions={1}, to_apply=%bitcast.132.reduce_sub_computation | reduce | bytes 524290
  104.8 3.8 %all-to-all-start.8 = ((bf16[16,2,4096]{2,1,0:T(2,128)(2,1)}), bf16[16,2,4096]{2,1,0:T(2,128)(2,1)S(1)}, u32[]{:S(2)}, u32[]{:S(2)}) async-start(bf16[16,2,4096]{2,1,0:T(2,128)(2,1)} %reshape.297), calls=%async_computation.8 | async-start | bytes 524288 | tf_op jit(solution)/shard_map/all_to_all | solution.py:115
  108.6 1.2 fusion.8
  109.9 1.2 multiply_reduce_fusion.6
  111.5 2.9 %reduce.13 = bf16[1024,128]{1,0:T(8,128)(2,1)} reduce(bf16[1024,1,128]{2,1,0:T(2,128)(2,1)S(1)} %bitcast.152, bf16[]{:T(256)} %broadcast.116), dimensions={1}, to_apply=%bitcast.133.reduce_sub_computation | reduce | bytes 524290
  114.4 1.7 reshape.295
  116.9 1.4 all-to-all-done.8
  118.4 4.3 %all-to-all-start.7 = ((bf16[16,2,4096]{2,1,0:T(2,128)(2,1)}), bf16[16,2,4096]{2,1,0:T(2,128)(2,1)S(1)}, u32[]{:S(2)}, u32[]{:S(2)}) async-start(bf16[16,2,4096]{2,1,0:T(2,128)(2,1)} %reshape.295), calls=%async_computation.7 | async-start | bytes 524288 | tf_op jit(solution)/shard_map/all_to_all | solution.py:114
  123.6 2.2 %reduce.11 = bf16[1024,128]{1,0:T(8,128)(2,1)S(1)} reduce(bf16[1024,1,128]{2,1,0:T(2,128)(2,1)S(1)} %bitcast.151, bf16[]{:T(256)} %broadcast.116), dimensions={1}, to_apply=%bitcast.134.reduce_sub_computation | reduce | bytes 524290
  126.5 6.2 %all-to-all-done.7 = bf16[16,2,4096]{2,1,0:T(2,128)(2,1)S(1)} async-done(((bf16[16,2,4096]{2,1,0:T(2,128)(2,1)}), bf16[16,2,4096]{2,1,0:T(2,128)(2,1)S(1)}, u32[]{:S(2)}, u32[]{:S(2)}) %all-to-all-start.7) | async-done | bytes 262176 | tf_op jit(solution)/shard_map/all_to_all | solution.py:114
  132.7 3.5 %all-to-all-start.6 = ((bf16[16,2,4096]{2,1,0:T(2,128)(2,1)}), bf16[16,2,4096]{2,1,0:T(2,128)(2,1)S(1)}, u32[]{:S(2)}, u32[]{:S(2)}) async-start(bf16[16,2,4096]{2,1,0:T(2,128)(2,1)} %reshape.293), calls=%async_computation.6 | async-start | bytes 524288 | tf_op jit(solution)/shard_map/all_to_all | solution.py:113
  138.5 40.5 %psum.7 = f32[2,16]{1,0:T(2,128)} all-reduce(f32[2,16]{1,0:T(2,128)S(1)} %and_select_fusion), channel_id=1, replica_groups=mesh['seq'=16,'dp'=2] {'seq','dp'}, use_global_device_ids=true, to_apply=%region_12.13 | all-reduce | flops 32 | bytes 256 | tf_op jit(solution)/shard_map/psum | solution.py:134
  (119 shorter events, 23.6 us)
Async XLA Ops:
  0.6 9.3 %copy-start.21 = (bf16[2,64,1024]{2,1,0:T(8,128)(2,1)S(1)}, bf16[2,64,1024]{2,1,0:T(8,128)(2,1)}, u32[]{:S(2)}) copy-start(bf16[2,64,1024]{2,1,0:T(8,128)(2,1)} %param.19) | copy-start | bytes 786436
  0.6 10.1 %copy-start.22 = (bf16[2,64,1024]{2,1,0:T(8,128)(2,1)S(1)}, bf16[2,64,1024]{2,1,0:T(8,128)(2,1)}, u32[]{:S(2)}) copy-start(bf16[2,64,1024]{2,1,0:T(8,128)(2,1)} %param.20) | copy-start | bytes 786436
  0.7 10.2 %copy-start.23 = (bf16[2,64,1024]{2,1,0:T(8,128)(2,1)S(1)}, bf16[2,64,1024]{2,1,0:T(8,128)(2,1)}, u32[]{:S(2)}) copy-start(bf16[2,64,1024]{2,1,0:T(8,128)(2,1)} %param.21) | copy-start | bytes 786436
  2.5 17.4 %all-to-all-start = ((bf16[16,64,128]{2,1,0:T(8,128)(2,1)}), bf16[16,64,128]{2,1,0:T(8,128)(2,1)S(1)}, u32[]{:S(2)}, u32[]{:S(2)}) async-start(bf16[16,64,128]{2,1,0:T(8,128)(2,1)} %bitcast.1), calls=%async_computation | async-start | bytes 524288 | tf_op jit(solution)/shard_map/all_to_all | solution.py:97
  10.0 14.3 %copy-start.24 = (bf16[2,64,1024]{2,1,0:T(8,128)(2,1)S(1)}, bf16[2,64,1024]{2,1,0:T(8,128)(2,1)}, u32[]{:S(2)}) copy-start(bf16[2,64,1024]{2,1,0:T(8,128)(2,1)} %param.22) | copy-start | bytes 786436
  10.0 14.3 %copy-start.25 = (bf16[2,64,1024]{2,1,0:T(8,128)(2,1)S(1)}, bf16[2,64,1024]{2,1,0:T(8,128)(2,1)}, u32[]{:S(2)}) copy-start(bf16[2,64,1024]{2,1,0:T(8,128)(2,1)} %param.23) | copy-start | bytes 786436
  19.9 13.5 %all-to-all-start.1 = ((bf16[16,64,128]{2,1,0:T(8,128)(2,1)}), bf16[16,64,128]{2,1,0:T(8,128)(2,1)S(1)}, u32[]{:S(2)}, u32[]{:S(2)}) async-start(bf16[16,64,128]{2,1,0:T(8,128)(2,1)} %bitcast.4), calls=%async_computation.1 | async-start | bytes 524288 | tf_op jit(solution)/shard_map/all_to_all | solution.py:98
  33.4 13.5 %all-to-all-start.2 = ((bf16[16,64,128]{2,1,0:T(8,128)(2,1)}), bf16[16,64,128]{2,1,0:T(8,128)(2,1)S(1)}, u32[]{:S(2)}, u32[]{:S(2)}) async-start(bf16[16,64,128]{2,1,0:T(8,128)(2,1)} %bitcast.7), calls=%async_computation.2 | async-start | bytes 524288 | tf_op jit(solution)/shard_map/all_to_all | solution.py:100
  47.0 13.5 %copy-start.6 = (bf16[16,64,128]{2,1,0:T(8,128)(2,1)}, bf16[16,64,128]{2,1,0:T(8,128)(2,1)S(1)}, u32[]{:S(2)}) copy-start(bf16[16,64,128]{2,1,0:T(8,128)(2,1)S(1)} %all-to-all-done.2) | copy-start | bytes 786436
  47.0 13.5 %all-to-all-start.4 = ((bf16[16,64,128]{2,1,0:T(8,128)(2,1)}), bf16[16,64,128]{2,1,0:T(8,128)(2,1)S(1)}, u32[]{:S(2)}, u32[]{:S(2)}) async-start(bf16[16,64,128]{2,1,0:T(8,128)(2,1)} %bitcast.13), calls=%async_computation.4 | async-start | bytes 524288 | tf_op jit(solution)/shard_map/all_to_all | solution.py:102
  60.5 13.5 %all-to-all-start.3 = ((bf16[16,64,128]{2,1,0:T(8,128)(2,1)}), bf16[16,64,128]{2,1,0:T(8,128)(2,1)S(1)}, u32[]{:S(2)}, u32[]{:S(2)}) async-start(bf16[16,64,128]{2,1,0:T(8,128)(2,1)} %bitcast.10), calls=%async_computation.3 | async-start | bytes 524288 | tf_op jit(solution)/shard_map/all_to_all | solution.py:101
  64.7 22.8 %copy-start.26 = (bf16[8,64,128]{2,1,0:T(8,128)(2,1)}, bf16[8,64,128]{2,1,0:T(8,128)(2,1)S(1)}, u32[]{:S(2)}) copy-start(bf16[8,64,128]{2,1,0:T(8,128)(2,1)S(1)} %get-tuple-element.83) | copy-start | bytes 393220
  74.0 7.4 %copy-start.3 = (bf16[16,64,128]{2,1,0:T(8,128)(2,1)}, bf16[16,64,128]{2,1,0:T(8,128)(2,1)S(1)}, u32[]{:S(2)}) copy-start(bf16[16,64,128]{2,1,0:T(8,128)(2,1)S(1)} %all-to-all-done.3) | copy-start | bytes 786436
  74.0 13.5 %all-to-all-start.5 = ((bf16[16,64,128]{2,1,0:T(8,128)(2,1)}), bf16[16,64,128]{2,1,0:T(8,128)(2,1)S(1)}, u32[]{:S(2)}, u32[]{:S(2)}) async-start(bf16[16,64,128]{2,1,0:T(8,128)(2,1)} %bitcast.16), calls=%async_computation.5 | async-start | bytes 524288 | tf_op jit(solution)/shard_map/all_to_all | solution.py:99
  87.5 2.7 %copy-start.16 = (bf16[16,64,128]{2,1,0:T(8,128)(2,1)}, bf16[16,64,128]{2,1,0:T(8,128)(2,1)S(1)}, u32[]{:S(2)}) copy-start(bf16[16,64,128]{2,1,0:T(8,128)(2,1)S(1)} %all-to-all-done.5) | copy-start | bytes 786436
  87.5 2.7 %copy-start.10 = (f32[512,1024]{1,0:T(8,128)S(1)}, f32[512,1024]{1,0:T(8,128)}, u32[]{:S(2)}) copy-start(f32[512,1024]{1,0:T(8,128)} %get-tuple-element.87) | copy-start | bytes 6291460
  91.5 2.5 %copy-start.11 = (bf16[8,64,128]{2,1,0:T(8,128)(2,1)S(1)}, bf16[8,64,128]{2,1,0:T(8,128)(2,1)}, u32[]{:S(2)}) copy-start(bf16[8,64,128]{2,1,0:T(8,128)(2,1)} %get-tuple-element.78) | copy-start | bytes 393220
  91.5 2.8 %copy-start.20 = (bf16[8,64,128]{2,1,0:T(8,128)(2,1)S(1)}, bf16[8,64,128]{2,1,0:T(8,128)(2,1)}, u32[]{:S(2)}) copy-start(bf16[8,64,128]{2,1,0:T(8,128)(2,1)} %get-tuple-element.80) | copy-start | bytes 393220
  97.3 2.4 %copy-start.27 = (bf16[8,64,128]{2,1,0:T(8,128)(2,1)S(1)}, bf16[8,64,128]{2,1,0:T(8,128)(2,1)}, u32[]{:S(2)}) copy-start(bf16[8,64,128]{2,1,0:T(8,128)(2,1)} %copy-done.26) | copy-start | bytes 393220
  100.9 7.7 %copy-start.2 = (bf16[512,512]{0,1:T(8,128)(2,1)S(1)}, bf16[512,512]{0,1:T(8,128)(2,1)}, u32[]{:S(2)}) copy-start(bf16[512,512]{0,1:T(8,128)(2,1)} %get-tuple-element.74) | copy-start | bytes 1572868
  100.9 7.7 %copy-start.12 = (bf16[8,64,128]{2,1,0:T(8,128)(2,1)S(1)}, bf16[8,64,128]{2,1,0:T(8,128)(2,1)}, u32[]{:S(2)}) copy-start(bf16[8,64,128]{2,1,0:T(8,128)(2,1)} %get-tuple-element.78) | copy-start | bytes 393220
  100.9 9.0 %copy-start.5 = (bf16[16,64,128]{2,1,0:T(8,128)(2,1)S(1)}, bf16[16,64,128]{2,1,0:T(8,128)(2,1)}, u32[]{:S(2)}) copy-start(bf16[16,64,128]{2,1,0:T(8,128)(2,1)} %copy-done.3) | copy-start | bytes 786436
  100.9 9.0 %copy-start.9 = (f32[1024,128]{1,0:T(8,128)S(1)}, f32[1024,128]{1,0:T(8,128)}, u32[]{:S(2)}) copy-start(f32[1024,128]{1,0:T(8,128)} %fusion.28) | copy-start | bytes 1572868
  100.9 9.0 %copy-start.14 = (bf16[8,64,128]{2,1,0:T(8,128)(2,1)S(1)}, bf16[8,64,128]{2,1,0:T(8,128)(2,1)}, u32[]{:S(2)}) copy-start(bf16[8,64,128]{2,1,0:T(8,128)(2,1)} %copy-done.13) | copy-start | bytes 393220
  104.8 13.5 %all-to-all-start.8 = ((bf16[16,2,4096]{2,1,0:T(2,128)(2,1)}), bf16[16,2,4096]{2,1,0:T(2,128)(2,1)S(1)}, u32[]{:S(2)}, u32[]{:S(2)}) async-start(bf16[16,2,4096]{2,1,0:T(2,128)(2,1)} %reshape.297), calls=%async_computation.8 | async-start | bytes 524288 | tf_op jit(solution)/shard_map/all_to_all | solution.py:115
  109.9 6.2 %copy-start.1 = (bf16[512,512]{0,1:T(8,128)(2,1)S(1)}, bf16[512,512]{0,1:T(8,128)(2,1)}, u32[]{:S(2)}) copy-start(bf16[512,512]{0,1:T(8,128)(2,1)} %copy-done) | copy-start | bytes 1572868
  111.1 5.4 %copy-start.15 = (f32[512,128]{1,0:T(8,128)S(1)}, f32[512,128]{1,0:T(8,128)}, u32[]{:S(2)}) copy-start(f32[512,128]{1,0:T(8,128)} %fusion.26) | copy-start | bytes 786436
  116.5 6.2 %copy-start.19 = (bf16[8,64,128]{2,1,0:T(8,128)(2,1)S(1)}, bf16[8,64,128]{2,1,0:T(8,128)(2,1)}, u32[]{:S(2)}) copy-start(bf16[8,64,128]{2,1,0:T(8,128)(2,1)} %copy-done.18) | copy-start | bytes 393220
  118.4 14.3 %all-to-all-start.7 = ((bf16[16,2,4096]{2,1,0:T(2,128)(2,1)}), bf16[16,2,4096]{2,1,0:T(2,128)(2,1)S(1)}, u32[]{:S(2)}, u32[]{:S(2)}) async-start(bf16[16,2,4096]{2,1,0:T(2,128)(2,1)} %reshape.295), calls=%async_computation.7 | async-start | bytes 524288 | tf_op jit(solution)/shard_map/all_to_all | solution.py:114
  123.1 13.2 %copy-start.7 = (bf16[16,64,128]{2,1,0:T(8,128)(2,1)S(1)}, bf16[16,64,128]{2,1,0:T(8,128)(2,1)}, u32[]{:S(2)}) copy-start(bf16[16,64,128]{2,1,0:T(8,128)(2,1)} %copy-done.6) | copy-start | bytes 786436
  123.1 15.3 %copy-start.29 = (pred[16]{0:T(512)(128)(4,1)S(1)}, pred[16]{0:T(512)(128)(4,1)}, u32[]{:S(2)}) copy-start(pred[16]{0:T(512)(128)(4,1)} %iota_compare_fusion.2) | copy-start | bytes 52
  132.7 47.0 %all-to-all-start.6 = ((bf16[16,2,4096]{2,1,0:T(2,128)(2,1)}), bf16[16,2,4096]{2,1,0:T(2,128)(2,1)S(1)}, u32[]{:S(2)}, u32[]{:S(2)}) async-start(bf16[16,2,4096]{2,1,0:T(2,128)(2,1)} %reshape.293), calls=%async_computation.6 | async-start | bytes 524288 | tf_op jit(solution)/shard_map/all_to_all | solution.py:113
  (7 other events, 7.9 us)
where the time goes:
time: 183 us; the launch traced here: 182 us
  waiting for transfers between devices  53.8 us (29%)
  blocking collectives  40.5 us (22%)
  starting transfers between devices  36.8 us (20%)
  local copies, waits for them, and re-layouts  18.6 us (10%)
  matrix products  17.2 us (9%)
  other arithmetic  12 us (7%)
  between operations  2.68 us (1%)
    psum x1, blocking collectives, local(): curvature = lax.psum(board, ('seq', 'dp'))  40.5 us
    unnamed x76, local copies, waits for them, and re-layouts  9.05 us
    all_to_all x1, waiting for transfers between devices, local(): lax.all_to_all(to_items(queries), 'seq', split_axis=0, concat_axis=1, til...  9 us
    all_to_all x1, waiting for transfers between devices, local(): lax.all_to_all(to_items(key_rows), 'seq', split_axis=0, concat_axis=1, ti...  9 us
    all_to_all x1, waiting for transfers between devices, local(): lax.all_to_all(to_items(key_tangent), 'seq', split_axis=0, concat_axis=1,...  8.73 us
    dot_general x8, matrix products, inner_rows(): lax.dot_general(left, right, (((1,), (1,)), ((), ())), preferred_element_...  8.68 us
    all_to_all x1, starting transfers between devices, local(): lax.all_to_all(to_items(queries), 'seq', split_axis=0, concat_axis=1, til...  7.39 us
    unnamed x3, other arithmetic  7.33 us
  transfers between devices with their start and end apart: 9, of which 8 were waited for; matrix products, arithmetic and copies ran while one was open for 14% of the time, Pallas kernels for 0%

commit v1 on v0

v1 whole, which is shorter than its diff:
```python
import functools
import math

import jax
import jax.numpy as jnp
from jax import lax
from jax.experimental import pallas as pl
from jax.experimental.pallas import tpu as pltpu
from jax.sharding import PartitionSpec as P

HEAD_DIM = 128
ROWS = 256
MESH = pl.DeviceIdType.MESH
F32 = jnp.float32
BF16 = jnp.bfloat16


def mm(left, right, dims):
    return lax.dot_general(left, right, (dims, ((), ())), preferred_element_type=F32)


def kernel(
    n,
    m,
    batch,
    local_heads,
    q_in,
    k_in,
    v_in,
    tq_in,
    tk_in,
    g_in,
    q_out,
    k_out,
    v_out,
    curv_out,
    qq,
    kk,
    gg,
    vv,
    probs_buf,
    tprobs_buf,
    hk_acc,
    hv_acc,
    staged,
    mine,
    board,
    in_send,
    in_recv,
    out_send,
    out_recv,
    board_send,
    board_recv,
):
    D = HEAD_DIM
    me = lax.axis_index("seq")
    dp = lax.axis_index("dp")
    tokens = q_in.shape[1]
    length = n * tokens
    rows = min(ROWS, length)
    blocks = length // rows
    per_block = rows // tokens
    factor = D ** (-0.5)

    barrier = pltpu.get_barrier_semaphore()

    def greet(step, carry):
        other = lax.rem(dp * n + me + step, n * m)
        pl.semaphore_signal(
            barrier, inc=1, device_id=(other % n, other // n), device_id_type=MESH
        )
        return carry

    lax.fori_loop(1, n * m, greet, 0)

    order = (
        (q_in, qq, D),
        (k_in, kk, 0),
        (tq_in, qq, 0),
        (tk_in, kk, D),
        (v_in, vv, 0),
        (g_in, gg, 0),
    )

    def landing(number, owner):
        _, buf, column = order[number]
        return buf.at[pl.ds(pl.multiple_of(owner * tokens, tokens), tokens), column : column + D]

    def piece(number, pair):
        source = order[number][0]
        b = pair // local_heads
        h = pair % local_heads
        return source.at[b, :, pl.ds(pl.multiple_of(h * D, D), D)]

    for number in range(6):
        pltpu.make_async_copy(piece(number, me), landing(number, me), in_recv.at[number]).start()

    pl.semaphore_wait(barrier, n * m - 1)

    def far_first(step):
        half = (step + 1) // 2
        hop = n // 2 + half * (1 - 2 * (step % 2))
        return (me + hop) % n

    for number in range(6):

        def send(step, carry, number=number):
            other = far_first(step)
            pltpu.make_async_remote_copy(
                src_ref=piece(number, other),
                dst_ref=landing(number, me),
                send_sem=in_send.at[number],
                recv_sem=in_recv.at[number],
                device_id=(other, dp),
                device_id_type=MESH,
            ).start()
            return carry

        lax.fori_loop(0, n - 1, send, 0)

    def arrived(number):
        _, buf, column = order[number]
        whole = buf.at[:, column : column + D]
        pltpu.make_async_copy(whole, whole, in_recv.at[number]).wait()

    my_batch = me // local_heads
    my_head = me % local_heads
    my_columns = pl.ds(pl.multiple_of(my_head * D, D), D)
    outs = (q_out, k_out, v_out)

    arrived(0)
    arrived(1)
    for block in range(blocks):
        start = block * rows
        width = start + rows
        part = slice(start, width)
        scores = mm(qq[part, D:], kk[:width, :D], ((1,), (1,)))
        row = lax.broadcasted_iota(jnp.int32, (rows, width), 0) + start
        col = lax.broadcasted_iota(jnp.int32, (rows, width), 1)
        scores = jnp.where(row >= col, scores, -jnp.inf)
        top = jnp.max(scores, axis=1, keepdims=True)
        weights = jnp.exp2((scores - top) * (factor * math.log2(math.e)))
        scale = 1.0 / jnp.sum(weights, axis=1, keepdims=True)
        probs_buf[part, :width] = weights * scale

    arrived(2)
    arrived(3)
    for block in range(blocks):
        start = block * rows
        width = start + rows
        part = slice(start, width)
        probs = probs_buf[part, :width]
        tangent = factor * mm(qq[part, :], kk[:width, :], ((1,), (1,)))
        mean = jnp.sum(probs * tangent, axis=1, keepdims=True)
        tprobs_buf[part, :width] = probs * (tangent - mean)

    arrived(4)
    arrived(5)
    kappa = jnp.zeros((1, 1), F32)
    for block in reversed(range(blocks)):
        start = block * rows
        width = start + rows
        part = slice(start, width)
        probs = probs_buf[part, :width]
        tprobs = tprobs_buf[part, :width]
        adj = gg[part, :]
        gprobs = mm(adj, vv[:width, :], ((1,), (1,)))
        delta = jnp.sum(probs * gprobs, axis=1, keepdims=True)
        centered = gprobs - delta
        tdelta = jnp.sum(tprobs * gprobs, axis=1, keepdims=True)
        tprob_low = tprobs.astype(BF16)
        gscore_low = (probs * centered).astype(BF16)
        second_low = (tprobs * centered - probs * tdelta).astype(BF16)
        hv = mm(tprob_low, adj, ((0,), (0,)))
        hq = factor * (
            mm(second_low, kk[:width, :D], ((1,), (0,)))
            + mm(gscore_low, kk[:width, D:], ((1,), (0,)))
        )
        hk = factor * (
            mm(second_low, qq[part, D:], ((0,), (0,)))
            + mm(gscore_low, qq[part, :D], ((0,), (0,)))
        )
        if block == blocks - 1:
            hk_acc[...] = hk
            hv_acc[...] = hv
        else:
            hk_acc[:width, :] += hk
            hv_acc[:width, :] += hv
        hk_done = hk_acc[part, :]
        kappa += jnp.sum(
            qq[part, :D].astype(F32) * hq + kk[part, D:].astype(F32) * hk_done, keepdims=True
        )
        staged[0, part, :] = hq.astype(BF16)
        staged[1, part, :] = hk_done.astype(BF16)
        staged[2, part, :] = hv_acc[part, :].astype(BF16)

        def give(step, carry, block=block):
            other = block * per_block + step
            mine_rows = pl.ds(pl.multiple_of(other * tokens, tokens), tokens)

            @pl.when(other == me)
            def _():
                for number in range(3):
                    pltpu.make_async_copy(
                        staged.at[number, mine_rows, :],
                        outs[number].at[my_batch, :, my_columns],
                        out_recv.at[number],
                    ).start()

            @pl.when(other != me)
            def _():
                for number in range(3):
                    pltpu.make_async_remote_copy(
                        src_ref=staged.at[number, mine_rows, :],
                        dst_ref=outs[number].at[my_batch, :, my_columns],
                        send_sem=out_send.at[number],
                        recv_sem=out_recv.at[number],
                        device_id=(other, dp),
                        device_id_type=MESH,
                    ).start()

            return carry

        lax.fori_loop(0, per_block, give, 0)

    shape = mine.shape
    at_row = lax.broadcasted_iota(jnp.int32, shape, 0) == my_batch
    at_col = lax.broadcasted_iota(jnp.int32, shape, 1) == dp * local_heads + my_head
    mine[...] = jnp.where(jnp.logical_and(at_row, at_col), kappa, 0.0)
    slot = dp * n + me

    def tell(step, carry):
        other = (slot + step) % (n * m)
        pltpu.make_async_remote_copy(
            src_ref=mine,
            dst_ref=board.at[slot],
            send_sem=board_send,
            recv_sem=board_recv,
            device_id=(other % n, other // n),
            device_id_type=MESH,
        ).start()
        return carry

    pltpu.make_async_copy(mine, board.at[slot], board_recv).start()
    lax.fori_loop(1, n * m, tell, 0)

    for number in range(6):
        _, buf, column = order[number]
        gone = buf.at[: (n - 1) * tokens, column : column + D]
        pltpu.make_async_copy(gone, gone, in_send.at[number]).wait()
    for number in range(3):
        gone = staged.at[number, : (n - 1) * tokens, :]
        pltpu.make_async_copy(gone, gone, out_send.at[number]).wait()
    gone = board.at[: n * m - 1]
    pltpu.make_async_copy(gone, gone, board_send).wait()
    pltpu.make_async_copy(board, board, board_recv).wait()
    total = jnp.sum(board[...], axis=0)
    curv_out[...] = total[: curv_out.shape[0], : curv_out.shape[1]]
    for number in range(3):
        pltpu.make_async_copy(outs[number], outs[number], out_recv.at[number]).wait()


def local(n, m, queries, key_rows, value_rows, query_tangent, key_tangent, out_adjoint):
    batch, tokens, width = queries.shape
    local_heads = width // HEAD_DIM
    length = n * tokens
    heads = local_heads * m
    board_shape = (-(-batch // 8) * 8, -(-heads // 128) * 128)
    result = jax.ShapeDtypeStruct(queries.shape, BF16)
    D = HEAD_DIM
    return pl.pallas_call(
        functools.partial(kernel, n, m, batch, local_heads),
        out_shape=(result, result, result, jax.ShapeDtypeStruct((batch, heads), F32)),
        in_specs=[pl.BlockSpec(memory_space=pl.ANY)] * 6,
        out_specs=(
            pl.BlockSpec(memory_space=pl.ANY),
            pl.BlockSpec(memory_space=pl.ANY),
            pl.BlockSpec(memory_space=pl.ANY),
            pl.BlockSpec(memory_space=pltpu.VMEM),
        ),
        scratch_shapes=[
            pltpu.VMEM((length, 2 * D), BF16),
            pltpu.VMEM((length, 2 * D), BF16),
            pltpu.VMEM((length, D), BF16),
            pltpu.VMEM((length, D), BF16),
            pltpu.VMEM((length, length), F32),
            pltpu.VMEM((length, length), F32),
            pltpu.VMEM((length, D), F32),
            pltpu.VMEM((length, D), F32),
            pltpu.VMEM((3, length, D), BF16),
            pltpu.VMEM(board_shape, F32),
            pltpu.VMEM((n * m,) + board_shape, F32),
            pltpu.SemaphoreType.DMA((6,)),
            pltpu.SemaphoreType.DMA((6,)),
            pltpu.SemaphoreType.DMA((3,)),
            pltpu.SemaphoreType.DMA((3,)),
            pltpu.SemaphoreType.DMA,
            pltpu.SemaphoreType.DMA,
        ],
        compiler_params=pltpu.CompilerParams(
            collective_id=0, has_side_effects=True, vmem_limit_bytes=56 * 1024 * 1024
        ),
    )(queries, key_rows, value_rows, query_tangent, key_tangent, out_adjoint)


def solution(mesh):
    split = P(None, "seq", "dp")
    return jax.shard_map(
        functools.partial(local, mesh.shape["seq"], mesh.shape["dp"]),
        mesh=mesh,
        in_specs=(split,) * 6,
        out_specs=(split, split, split, P()),
        check_vma=False,
    )
```

time: 183 us -> 74 us (0.40)
  Pallas kernels: 0 us -> 69.1 us
  waiting for transfers between devices: 53.8 us -> 0 us
  blocking collectives: 40.5 us -> 0 us
  starting transfers between devices: 36.8 us -> 0 us
  matrix products: 17.2 us -> 0 us
  local copies, waits for them, and re-layouts: 18.6 us -> 4.03 us
  other arithmetic: 12 us -> 0 us
  between operations: 2.68 us -> 0.65 us
    pallas_call x0 -> x1, Pallas kernels: none -> 69.1 us  [local(): pl.pallas_call(functools.partial(kernel, n, m, batch, local_heads), out_s...]
    all_to_all x9 -> x0, waiting for transfers between devices: 53.8 us -> none  [the longest x1 9 us: local(): lax.all_to_all(to_items(queries), 'seq', split_axis=0, concat_axis=1, til...]
    psum x1 -> x0, blocking collectives: 40.5 us -> none  [local(): curvature = lax.psum(board, ('seq', 'dp'))]
    all_to_all x9 -> x0, starting transfers between devices: 36.8 us -> none  [the longest x1 7.39 us: local(): lax.all_to_all(to_items(queries), 'seq', split_axis=0, concat_axis=1, til...]
    dot_general x18 -> x0, matrix products: 17.2 us -> none  [the longest x8 8.68 us: inner_rows(): lax.dot_general(left, right, (((1,), (1,)), ((), ())), preferred_element_...]
    unnamed x3 -> x0, other arithmetic: 7.33 us -> none
    unnamed x76 -> x10, local copies, waits for them, and re-layouts: 9.05 us -> 4.03 us
    transpose x12 -> x0, local copies, waits for them, and re-layouts: 4.64 us -> none  [to_items(): jnp.transpose(shaped, (0, 2, 1, 3))]
  transfers between devices with their start and end apart: 9 -> 0, of which waited for: 8 -> 0; matrix products, arithmetic and copies ran while one was open for 14% -> 0% of each run, Pallas kernels for 0% -> 0%
where the time goes in v1:
time: 74 us; the launch traced here: 73.8 us
  Pallas kernels  69.1 us (93%)
  local copies, waits for them, and re-layouts  4.03 us (5%)
    pallas_call x1, Pallas kernels, local(): pl.pallas_call(functools.partial(kernel, n, m, batch, local_heads), out_s...  69.1 us
    unnamed x10, local copies, waits for them, and re-layouts  4.03 us

profile of v1, /device:TPU:0, one launch (start us, length us, event | category | flops | bytes accessed | tf_op | source)
XLA Modules:
  0.0 73.8 jit_solution(17175262706719192067)
XLA Ops:
  0.6 69.1 %shard_map.93 = (bf16[2,64,1024]{2,1,0:T(8,128)(2,1)}, bf16[2,64,1024]{2,1,0:T(8,128)(2,1)}, bf16[2,64,1024]{2,1,0:T(8,128)(2,1)}, f32[2,16]{1,0:T(2,128)}) custom-call(bf16[2,64,1024]{2,1,0:T(8,128)(2,1)} %q_in.1, bf16[2,64,1024]{2,1,0:T(8,128)(2,1)} %k_in.1, bf16[2,64,1024]{2,1,0:T(8,128)(2,1)} %v_in.1, bf16[2,64,1024]{2,1,0:T(8,128)(2,1)} %tq_in.1, ...), custom_call_target="tpu_custom_call" | custom-call | tf_op jit(solution)/shard_map/pallas_call | solution.py:271
  69.8 0.0 copy-start.1
  69.8 1.7 %copy.14 = bf16[2,64,1024]{2,1,0:T(8,128)(2,1)} copy(bf16[2,64,1024]{2,1,0:T(8,128)(2,1)} %get-tuple-element.8) | data formatting | bytes 524288
  71.5 0.0 copy-done.1
  71.5 0.0 copy-start
  71.5 0.7 copy.15
  72.2 0.3 copy-done
  72.6 0.0 copy-start.2
  72.6 0.7 copy.16
  73.3 0.0 copy-done.2
  73.3 0.6 copy.17
Async XLA Ops:
  69.8 1.7 %copy-start.1 = (bf16[2,64,1024]{2,1,0:T(8,128)(2,1)S(1)}, bf16[2,64,1024]{2,1,0:T(8,128)(2,1)}, u32[]{:S(2)}) copy-start(bf16[2,64,1024]{2,1,0:T(8,128)(2,1)} %get-tuple-element.9) | copy-start | bytes 786436
  71.5 1.0 %copy-start = (bf16[2,64,1024]{2,1,0:T(8,128)(2,1)S(1)}, bf16[2,64,1024]{2,1,0:T(8,128)(2,1)}, u32[]{:S(2)}) copy-start(bf16[2,64,1024]{2,1,0:T(8,128)(2,1)} %get-tuple-element.10) | copy-start | bytes 786436
  72.6 0.7 copy-start.2

commit v2 on v1

v2 whole, which is shorter than its diff:
```python
import functools
import math

import jax
import jax.numpy as jnp
from jax import lax
from jax.experimental import pallas as pl
from jax.experimental.pallas import tpu as pltpu
from jax.sharding import PartitionSpec as P

HEAD_DIM = 128
ROWS = 256
SLOTS = 3
MESH = pl.DeviceIdType.MESH
F32 = jnp.float32
BF16 = jnp.bfloat16


def mm(left, right, dims):
    return lax.dot_general(left, right, (dims, ((), ())), preferred_element_type=F32)


def kernel(
    n,
    m,
    local_heads,
    q_in,
    k_in,
    v_in,
    tq_in,
    tk_in,
    g_in,
    q_out,
    k_out,
    v_out,
    curv_out,
    qq,
    kk,
    gg,
    vv,
    hk_acc,
    hv_acc,
    q_staged,
    k_staged,
    v_staged,
    k_low,
    v_low,
    mine,
    board,
    in_send,
    in_recv,
    out_send,
    out_recv,
    low_recv,
    board_send,
    board_recv,
):
    D = HEAD_DIM
    me = lax.axis_index("seq")
    dp = lax.axis_index("dp")
    tokens = q_in.shape[1]
    quarter = n // 4
    half = n // 2
    length = n * tokens
    upper = half * tokens
    rows = min(ROWS, upper)
    per_block = rows // tokens
    factor = D ** (-0.5)
    level = me // quarter
    ring = me % quarter
    near = ((level + 1) // 2) % 2
    low = level < 2
    slots = 1 + (SLOTS - 1) * near

    barrier = pltpu.get_barrier_semaphore()

    def greet(step, carry):
        other = lax.rem(dp * n + me + step, n * m)
        pl.semaphore_signal(
            barrier, inc=1, device_id=(other % n, other // n), device_id_type=MESH
        )
        return carry

    lax.fori_loop(1, n * m, greet, 0)

    tensors = (
        (k_in, kk, 0, length),
        (tk_in, kk, D, length),
        (v_in, vv, 0, length),
        (q_in, qq, D, upper),
        (tq_in, qq, 0, upper),
        (g_in, gg, 0, upper),
    )

    def columns(pair):
        return pl.ds(pl.multiple_of((pair % local_heads) * D, D), D)

    def feed(number, pair, slot, home, row):
        source, buf, column, span = tensors[number]
        src = source.at[pair // local_heads, :, columns(pair)]
        at = pl.multiple_of(slot * span + row, tokens)
        dst = buf.at[pl.ds(at, tokens), column : column + D]

        @pl.when(home == me)
        def _():
            pltpu.make_async_copy(src, dst, in_recv.at[slot, number]).start()

        @pl.when(home != me)
        def _():
            pltpu.make_async_remote_copy(
                src_ref=src,
                dst_ref=dst,
                send_sem=in_send.at[number],
                recv_sem=in_recv.at[slot, number],
                device_id=(home, dp),
                device_id_type=MESH,
            ).start()

    pl.semaphore_wait(barrier, n * m - 1)

    for group in (0, 3, 1, 2):
        far = 1 if group == 3 else 0
        slot = 0 if far else group

        def send(step, carry, group=group, far=far, slot=slot):
            spot = (me + step) % quarter
            pair = group * quarter + spot
            low_home = (1 - far) * quarter + spot
            high_home = half + far * quarter + spot

            @pl.when(low)
            def _():
                for number in range(3):
                    feed(number, pair, slot, high_home, me * tokens)
                for number in range(6):
                    feed(number, pair, slot, low_home, me * tokens)

            @pl.when(jnp.logical_not(low))
            def _():
                for number in range(3):
                    feed(number, pair, slot, high_home, me * tokens)
                for number in range(3, 6):
                    feed(number, pair, slot, high_home, (me - half) * tokens)

            return carry

        lax.fori_loop(0, quarter, send, 0)

    shape = mine.shape
    mine[...] = jnp.zeros(shape, F32)

    def ship(staged, at, other, dst, number, recv):
        src = staged.at[pl.ds(pl.multiple_of(at, tokens), tokens), :]

        @pl.when(other == me)
        def _():
            pltpu.make_async_copy(src, dst, recv).start()

        @pl.when(other != me)
        def _():
            pltpu.make_async_remote_copy(
                src_ref=src,
                dst_ref=dst,
                send_sem=out_send.at[number],
                recv_sem=recv,
                device_id=(other, dp),
                device_id_type=MESH,
            ).start()

    def work(slot, base):
        group = near * slot + (1 - near) * 3
        pair = group * quarter + ring
        batch = pair // local_heads
        cols = columns(pair)
        keys = base + upper
        top_rows = pl.multiple_of(slot * upper, rows)
        top_keys = pl.multiple_of(slot * length, rows)

        def arrived(number, count):
            _, buf, column, span = tensors[number]
            whole = buf.at[:count, column : column + D]
            pltpu.make_async_copy(whole, whole, in_recv.at[slot, number]).wait()

        for number in range(6):
            arrived(number, keys if number < 3 else upper)

        kappa = jnp.zeros((1, 1), F32)
        for start in reversed(range(base, keys, rows)):
            width = start + rows
            here = pl.ds(pl.multiple_of(top_rows + (start - base), rows), rows)
            seen = pl.ds(top_keys, width)
            both = qq[here, :]
            adj = gg[here, :]
            both_keys = kk[seen, :]
            scores = mm(both[:, D:], both_keys[:, :D], ((1,), (1,)))
            row = lax.broadcasted_iota(jnp.int32, (rows, width), 0) + start
            col = lax.broadcasted_iota(jnp.int32, (rows, width), 1)
            scores = jnp.where(row >= col, scores, -jnp.inf)
            top = jnp.max(scores, axis=1, keepdims=True)
            weights = jnp.exp2((scores - top) * (factor * math.log2(math.e)))
            probs = weights * (1.0 / jnp.sum(weights, axis=1, keepdims=True))
            tangent = factor * mm(both, both_keys, ((1,), (1,)))
            mean = jnp.sum(probs * tangent, axis=1, keepdims=True)
            tprobs = probs * (tangent - mean)
            gprobs = mm(adj, vv[seen, :], ((1,), (1,)))
            delta = jnp.sum(probs * gprobs, axis=1, keepdims=True)
            centered = gprobs - delta
            tdelta = jnp.sum(tprobs * gprobs, axis=1, keepdims=True)
            tprob_low = tprobs.astype(BF16)
            gscore_low = (probs * centered).astype(BF16)
            second_low = (tprobs * centered - probs * tdelta).astype(BF16)
            hv = mm(tprob_low, adj, ((0,), (0,)))
            hq = factor * (
                mm(second_low, both_keys[:, :D], ((1,), (0,)))
                + mm(gscore_low, both_keys[:, D:], ((1,), (0,)))
            )
            hk = factor * (
                mm(second_low, both[:, D:], ((0,), (0,)))
                + mm(gscore_low, both[:, :D], ((0,), (0,)))
            )
            if width == keys:
                hk_acc[:keys, :] = hk
                hv_acc[:keys, :] = hv
            else:
                hk_acc[:width, :] += hk
                hv_acc[:width, :] += hv
            kappa += jnp.sum(both[:, :D].astype(F32) * hq, keepdims=True)
            q_staged[here, :] = hq.astype(BF16)

            done = start if start > base else 0
            count = width - done
            span = slice(done, width)
            area = pl.ds(pl.multiple_of(top_keys + done, rows), count)
            hk_done = hk_acc[span, :]
            kappa += jnp.sum(kk[area, D:].astype(F32) * hk_done, keepdims=True)
            k_staged[area, :] = hk_done.astype(BF16)
            v_staged[area, :] = hv_acc[span, :].astype(BF16)

            def give_q(step, carry, start=start):
                other = start // tokens + step
                at = top_rows + other * tokens - base
                ship(q_staged, at, other, q_out.at[batch, :, cols], 0, out_recv.at[0])
                return carry

            def give_kv(step, carry, done=done):
                other = done // tokens + step
                at = top_keys + other * tokens
                if base:
                    ship(k_staged, at, other, k_out.at[batch, :, cols], 1, out_recv.at[1])
                    ship(v_staged, at, other, v_out.at[batch, :, cols], 2, out_recv.at[2])
                else:
                    ship(k_staged, at, other, k_low.at[batch, :, cols], 1, low_recv.at[0])
                    ship(v_staged, at, other, v_low.at[batch, :, cols], 2, low_recv.at[1])
                return carry

            lax.fori_loop(0, count // tokens, give_kv, 0)
            lax.fori_loop(0, per_block, give_q, 0)

        at_row = lax.broadcasted_iota(jnp.int32, shape, 0) == batch
        at_col = (
            lax.broadcasted_iota(jnp.int32, shape, 1) == dp * local_heads + pair % local_heads
        )
        mine[...] += jnp.where(jnp.logical_and(at_row, at_col), kappa, 0.0)

    def all_slots(base):
        def one(slot, carry):
            work(slot, base)
            return carry

        lax.fori_loop(0, slots, one, 0)

    @pl.when(low)
    def _():
        all_slots(0)

    @pl.when(jnp.logical_not(low))
    def _():
        all_slots(upper)

    place = dp * n + me

    def tell(step, carry):
        other = (place + step) % (n * m)
        pltpu.make_async_remote_copy(
            src_ref=mine,
            dst_ref=board.at[place],
            send_sem=board_send,
            recv_sem=board_recv,
            device_id=(other % n, other // n),
            device_id_type=MESH,
        ).start()
        return carry

    pltpu.make_async_copy(mine, board.at[place], board_recv).start()
    lax.fori_loop(1, n * m, tell, 0)

    def gone(units, sem):
        sent = vv.at[: units * tokens, :]
        pltpu.make_async_copy(sent, sent, sem).wait()

    for is_low in (True, False):
        for count, is_near in ((SLOTS, 1), (1, 0)):

            @pl.when(jnp.logical_and(low == is_low, near == is_near))
            def _(is_low=is_low, count=count):
                for number in range(6):
                    gone(n - count + (n if is_low and number < 3 else 0), in_send.at[number])
                gone(count * (half - 1), out_send.at[0])
                for number in (1, 2):
                    gone(count * ((half if is_low else n) - 1), out_send.at[number])

    sent = board.at[: n * m - 1]
    pltpu.make_async_copy(sent, sent, board_send).wait()

    pltpu.make_async_copy(q_out, q_out, out_recv.at[0]).wait()
    pltpu.make_async_copy(k_out, k_out, out_recv.at[1]).wait()
    pltpu.make_async_copy(v_out, v_out, out_recv.at[2]).wait()

    @pl.when(low)
    def _():
        pltpu.make_async_copy(k_low, k_low, low_recv.at[0]).wait()
        pltpu.make_async_copy(v_low, v_low, low_recv.at[1]).wait()
        k_out[...] = (k_out[...].astype(F32) + k_low[...].astype(F32)).astype(BF16)
        v_out[...] = (v_out[...].astype(F32) + v_low[...].astype(F32)).astype(BF16)

    pltpu.make_async_copy(board, board, board_recv).wait()
    total = jnp.sum(board[...], axis=0)
    curv_out[...] = total[: curv_out.shape[0], : curv_out.shape[1]]


def local(n, m, queries, key_rows, value_rows, query_tangent, key_tangent, out_adjoint):
    batch, tokens, width = queries.shape
    local_heads = width // HEAD_DIM
    length = n * tokens
    heads = local_heads * m
    board_shape = (-(-batch // 8) * 8, -(-heads // 128) * 128)
    result = jax.ShapeDtypeStruct(queries.shape, BF16)
    D = HEAD_DIM
    return pl.pallas_call(
        functools.partial(kernel, n, m, local_heads),
        out_shape=(result, result, result, jax.ShapeDtypeStruct((batch, heads), F32)),
        in_specs=[pl.BlockSpec(memory_space=pl.ANY)] * 6,
        out_specs=(pl.BlockSpec(memory_space=pltpu.VMEM),) * 4,
        scratch_shapes=[
            pltpu.VMEM((SLOTS * length // 2, 2 * D), BF16),
            pltpu.VMEM((SLOTS * length, 2 * D), BF16),
            pltpu.VMEM((SLOTS * length // 2, D), BF16),
            pltpu.VMEM((SLOTS * length, D), BF16),
            pltpu.VMEM((length, D), F32),
            pltpu.VMEM((length, D), F32),
            pltpu.VMEM((SLOTS * length // 2, D), BF16),
            pltpu.VMEM((SLOTS * length, D), BF16),
            pltpu.VMEM((SLOTS * length, D), BF16),
            pltpu.VMEM(queries.shape, BF16),
            pltpu.VMEM(queries.shape, BF16),
            pltpu.VMEM(board_shape, F32),
            pltpu.VMEM((n * m,) + board_shape, F32),
            pltpu.SemaphoreType.DMA((6,)),
            pltpu.SemaphoreType.DMA((SLOTS, 6)),
            pltpu.SemaphoreType.DMA((3,)),
            pltpu.SemaphoreType.DMA((3,)),
            pltpu.SemaphoreType.DMA((2,)),
            pltpu.SemaphoreType.DMA,
            pltpu.SemaphoreType.DMA,
        ],
        compiler_params=pltpu.CompilerParams(
            collective_id=0, has_side_effects=True, vmem_limit_bytes=56 * 1024 * 1024
        ),
    )(queries, key_rows, value_rows, query_tangent, key_tangent, out_adjoint)


def solution(mesh):
    split = P(None, "seq", "dp")
    return jax.shard_map(
        functools.partial(local, mesh.shape["seq"], mesh.shape["dp"]),
        mesh=mesh,
        in_specs=(split,) * 6,
        out_specs=(split, split, split, P()),
        check_vma=False,
    )
```

time: 74 us -> 70.8 us (0.957)
  Pallas kernels: 69.1 us -> 66 us
    pallas_call x1, Pallas kernels: 69.1 us -> 66 us  [local(): pl.pallas_call(functools.partial(kernel, n, m, local_heads), out_shape=(r...]
where the time goes in v2:
time: 70.8 us; the launch traced here: 70.6 us
  Pallas kernels  66 us (93%)
  local copies, waits for them, and re-layouts  4.03 us (6%)
    pallas_call x1, Pallas kernels, local(): pl.pallas_call(functools.partial(kernel, n, m, local_heads), out_shape=(r...  66 us
    unnamed x10, local copies, waits for them, and re-layouts  4.03 us

profile of v2, /device:TPU:0, one launch (start us, length us, event | category | flops | bytes accessed | tf_op | source)
XLA Modules:
  0.0 70.6 jit_solution(6863656878300551359)
XLA Ops:
  0.6 66.0 %shard_map.93 = (bf16[2,64,1024]{2,1,0:T(8,128)(2,1)}, bf16[2,64,1024]{2,1,0:T(8,128)(2,1)}, bf16[2,64,1024]{2,1,0:T(8,128)(2,1)}, f32[2,16]{1,0:T(2,128)}) custom-call(bf16[2,64,1024]{2,1,0:T(8,128)(2,1)} %q_in.1, bf16[2,64,1024]{2,1,0:T(8,128)(2,1)} %k_in.1, bf16[2,64,1024]{2,1,0:T(8,128)(2,1)} %v_in.1, bf16[2,64,1024]{2,1,0:T(8,128)(2,1)} %tq_in.1, ...), custom_call_target="tpu_custom_call" | custom-call | tf_op jit(solution)/shard_map/pallas_call | solution.py:339
  66.6 0.0 copy-start.1
  66.6 1.7 %copy.14 = bf16[2,64,1024]{2,1,0:T(8,128)(2,1)} copy(bf16[2,64,1024]{2,1,0:T(8,128)(2,1)} %get-tuple-element.8) | data formatting | bytes 524288
  68.3 0.0 copy-done.1
  68.3 0.0 copy-start
  68.3 0.7 copy.15
  69.0 0.3 copy-done
  69.4 0.0 copy-start.2
  69.4 0.7 copy.16
  70.1 0.0 copy-done.2
  70.1 0.6 copy.17
Async XLA Ops:
  66.6 1.7 %copy-start.1 = (bf16[2,64,1024]{2,1,0:T(8,128)(2,1)S(1)}, bf16[2,64,1024]{2,1,0:T(8,128)(2,1)}, u32[]{:S(2)}) copy-start(bf16[2,64,1024]{2,1,0:T(8,128)(2,1)} %get-tuple-element.9) | copy-start | bytes 786436
  68.3 1.0 %copy-start = (bf16[2,64,1024]{2,1,0:T(8,128)(2,1)S(1)}, bf16[2,64,1024]{2,1,0:T(8,128)(2,1)}, u32[]{:S(2)}) copy-start(bf16[2,64,1024]{2,1,0:T(8,128)(2,1)} %get-tuple-element.10) | copy-start | bytes 786436
  69.4 0.7 %copy-start.2 = (f32[2,16]{1,0:T(2,128)S(1)}, f32[2,16]{1,0:T(2,128)}, u32[]{:S(2)}) copy-start(f32[2,16]{1,0:T(2,128)} %get-tuple-element.11) | copy-start | bytes 388

commit v3 on v2

--- a/solution.py
+++ b/solution.py
@@ -38,6 +38,7 @@
     kk,
     gg,
     vv,
+    relay,
     hk_acc,
     hv_acc,
     q_staged,
@@ -49,6 +50,7 @@
     board,
     in_send,
     in_recv,
+    relay_recv,
     out_send,
     out_recv,
     low_recv,
@@ -95,9 +97,11 @@
     def columns(pair):
         return pl.ds(pl.multiple_of((pair % local_heads) * D, D), D)
 
-    def feed(number, pair, slot, home, row):
-        source, buf, column, span = tensors[number]
-        src = source.at[pair // local_heads, :, columns(pair)]
+    def cut(number, pair):
+        return tensors[number][0].at[pair // local_heads, :, columns(pair)]
+
+    def feed(number, src, slot, home, row):
+        _, buf, column, span = tensors[number]
         at = pl.multiple_of(slot * span + row, tokens)
         dst = buf.at[pl.ds(at, tokens), column : column + D]
 
@@ -118,33 +122,76 @@
 
     pl.semaphore_wait(barrier, n * m - 1)
 
-    for group in (0, 3, 1, 2):
+    side = (me // 2) % 2
+    partner = (me // 4) * 4 + (me + 2) % 4
+
+    def spot_of(step, column):
+        return (step // 2) * 4 + 2 * column + step % 2
+
+    def swap(step, carry):
+        group = step // (quarter // 2)
+        pair = group * quarter + spot_of(step % (quarter // 2), 1 - side)
+        for number in range(6):
+            at = pl.multiple_of((step * 6 + number) * tokens, tokens)
+            pltpu.make_async_remote_copy(
+                src_ref=cut(number, pair),
+                dst_ref=relay.at[pl.ds(at, tokens), :],
+                send_sem=in_send.at[number],
+                recv_sem=relay_recv.at[group],
+                device_id=(partner, dp),
+                device_id_type=MESH,
+            ).start()
+        return carry
+
+    def forward(group, relayed):
         far = 1 if group == 3 else 0
         slot = 0 if far else group
-
-        def send(step, carry, group=group, far=far, slot=slot):
-            spot = (me + step) % quarter
+        owner = partner if relayed else me
+        first = group * (quarter // 2)
+        if relayed:
+            batch_of = 6 * (quarter // 2) * tokens
+            all_of = relay.at[group * batch_of : (group + 1) * batch_of, :]
+            pltpu.make_async_copy(all_of, all_of, relay_recv.at[group]).wait()
+
+        def send(step, carry):
+            spot = spot_of(step, side)
             pair = group * quarter + spot
             low_home = (1 - far) * quarter + spot
             high_home = half + far * quarter + spot
 
+            def source(number):
+                if relayed:
+                    at = pl.multiple_of(((first + step) * 6 + number) * tokens, tokens)
+                    return relay.at[pl.ds(at, tokens), :]
+                return cut(number, pair)
+
             @pl.when(low)
             def _():
                 for number in range(3):
-                    feed(number, pair, slot, high_home, me * tokens)
+                    feed(number, source(number), slot, high_home, owner * tokens)
                 for number in range(6):
-                    feed(number, pair, slot, low_home, me * tokens)
+                    feed(number, source(number), slot, low_home, owner * tokens)
 
             @pl.when(jnp.logical_not(low))
             def _():
                 for number in range(3):
-                    feed(number, pair, slot, high_home, me * tokens)
+                    feed(number, source(number), slot, high_home, owner * tokens)
                 for number in range(3, 6):
-                    feed(number, pair, slot, high_home, (me - half) * tokens)
+                    feed(number, source(number), slot, high_home, (owner - half) * tokens)
 
             return carry
 
-        lax.fori_loop(0, quarter, send, 0)
+        lax.fori_loop(0, quarter // 2, send, 0)
+
+    lax.fori_loop(0, half, swap, 0)
+    forward(0, False)
+    forward(3, False)
+    forward(0, True)
+    forward(3, True)
+    forward(1, False)
+    forward(1, True)
+    forward(2, False)
+    forward(2, True)
 
     shape = mine.shape
     mine[...] = jnp.zeros(shape, F32)
@@ -304,7 +351,7 @@
             @pl.when(jnp.logical_and(low == is_low, near == is_near))
             def _(is_low=is_low, count=count):
                 for number in range(6):
-                    gone(n - count + (n if is_low and number < 3 else 0), in_send.at[number])
+                    gone(n - 2 * count + half + (n if is_low and number < 3 else 0), in_send.at[number])
                 gone(count * (half - 1), out_send.at[0])
                 for number in (1, 2):
                     gone(count * ((half if is_low else n) - 1), out_send.at[number])
@@ -326,6 +373,28 @@
     pltpu.make_async_copy(board, board, board_recv).wait()
     total = jnp.sum(board[...], axis=0)
     curv_out[...] = total[: curv_out.shape[0], : curv_out.shape[1]]
+
+
+def hand_over(q, k, v, curv, q_out, k_out, v_out, curv_out, held, read, written):
+    batch = q.shape[0]
+    parts = [(number, b) for number in range(3) for b in range(batch)]
+    sources, outs = (q, k, v), (q_out, k_out, v_out)
+    reads, writes = [], []
+    for number, b in parts:
+        reads.append(
+            pltpu.make_async_copy(sources[number].at[b], held.at[number, b], read.at[number, b])
+        )
+        writes.append(
+            pltpu.make_async_copy(held.at[number, b], outs[number].at[b], written.at[number, b])
+        )
+    for copy in reads:
+        copy.start()
+    curv_out[...] = curv[...]
+    for first, second in zip(reads, writes):
+        first.wait()
+        second.start()
+    for copy in writes:
+        copy.wait()
 
 
 def local(n, m, queries, key_rows, value_rows, query_tangent, key_tangent, out_adjoint):
@@ -336,7 +405,7 @@
     board_shape = (-(-batch // 8) * 8, -(-heads // 128) * 128)
     result = jax.ShapeDtypeStruct(queries.shape, BF16)
     D = HEAD_DIM
-    return pl.pallas_call(
+    landed = pl.pallas_call(
         functools.partial(kernel, n, m, local_heads),
         out_shape=(result, result, result, jax.ShapeDtypeStruct((batch, heads), F32)),
         in_specs=[pl.BlockSpec(memory_space=pl.ANY)] * 6,
@@ -346,6 +415,7 @@
             pltpu.VMEM((SLOTS * length, 2 * D), BF16),
             pltpu.VMEM((SLOTS * length // 2, D), BF16),
             pltpu.VMEM((SLOTS * length, D), BF16),
+            pltpu.VMEM((3 * length, D), BF16),
             pltpu.VMEM((length, D), F32),
             pltpu.VMEM((length, D), F32),
             pltpu.VMEM((SLOTS * length // 2, D), BF16),
@@ -357,6 +427,7 @@
             pltpu.VMEM((n * m,) + board_shape, F32),
             pltpu.SemaphoreType.DMA((6,)),
             pltpu.SemaphoreType.DMA((SLOTS, 6)),
+            pltpu.SemaphoreType.DMA((4,)),
             pltpu.SemaphoreType.DMA((3,)),
             pltpu.SemaphoreType.DMA((3,)),
             pltpu.SemaphoreType.DMA((2,)),
@@ -367,6 +438,22 @@
             collective_id=0, has_side_effects=True, vmem_limit_bytes=56 * 1024 * 1024
         ),
     )(queries, key_rows, value_rows, query_tangent, key_tangent, out_adjoint)
+    return pl.pallas_call(
+        hand_over,
+        out_shape=(result, result, result, jax.ShapeDtypeStruct((batch, heads), F32)),
+        in_specs=[pl.BlockSpec(memory_space=pl.ANY)] * 3 + [pl.BlockSpec(memory_space=pltpu.VMEM)],
+        out_specs=(
+            pl.BlockSpec(memory_space=pl.ANY),
+            pl.BlockSpec(memory_space=pl.ANY),
+            pl.BlockSpec(memory_space=pl.ANY),
+            pl.BlockSpec(memory_space=pltpu.VMEM),
+        ),
+        scratch_shapes=[
+            pltpu.VMEM((3,) + queries.shape, BF16),
+            pltpu.SemaphoreType.DMA((3, batch)),
+            pltpu.SemaphoreType.DMA((3, batch)),
+        ],
+    )(*landed)
 
 
 def solution(mesh):

time: 70.8 us -> 72.3 us (1.021)
  Pallas kernels: 66 us -> 71.5 us
  local copies, waits for them, and re-layouts: 4.03 us -> 0 us
    unnamed x10 -> x0, local copies, waits for them, and re-layouts: 4.03 us -> none
    pallas_call x0 -> x1, Pallas kernels: none -> 3.19 us  [local(): pl.pallas_call(hand_over, out_shape=(result, result, result, jax.ShapeDty...]
    pallas_call x1, Pallas kernels: 66 us -> 68.3 us  [local(): pl.pallas_call(functools.partial(kernel, n, m, local_heads), out_shape=(r...]
where the time goes in v3:
time: 72.3 us; the launch traced here: 72.1 us
  Pallas kernels  71.5 us (99%)
    pallas_call x1, Pallas kernels, local(): pl.pallas_call(functools.partial(kernel, n, m, local_heads), out_shape=(r...  68.3 us
    pallas_call x1, Pallas kernels, local(): pl.pallas_call(hand_over, out_shape=(result, result, result, jax.ShapeDty...  3.19 us

profile of v3, /device:TPU:0, one launch (start us, length us, event | category | flops | bytes accessed | tf_op | source)
XLA Modules:
  0.0 72.1 jit_solution(8264841952401355256)
XLA Ops:
  0.6 68.3 %shard_map.93 = (bf16[2,64,1024]{2,1,0:T(8,128)(2,1)}, bf16[2,64,1024]{2,1,0:T(8,128)(2,1)}, bf16[2,64,1024]{2,1,0:T(8,128)(2,1)}, f32[2,16]{1,0:T(2,128)}) custom-call(bf16[2,64,1024]{2,1,0:T(8,128)(2,1)} %q_in.1, bf16[2,64,1024]{2,1,0:T(8,128)(2,1)} %k_in.1, bf16[2,64,1024]{2,1,0:T(8,128)(2,1)} %v_in.1, bf16[2,64,1024]{2,1,0:T(8,128)(2,1)} %tq_in.1, ...), custom_call_target="tpu_custom_call" | custom-call | tf_op jit(solution)/shard_map/pallas_call | solution.py:408
  68.9 3.2 %shard_map.94 = (bf16[2,64,1024]{2,1,0:T(8,128)(2,1)}, bf16[2,64,1024]{2,1,0:T(8,128)(2,1)}, bf16[2,64,1024]{2,1,0:T(8,128)(2,1)}, f32[2,16]{1,0:T(2,128)}) custom-call(bf16[2,64,1024]{2,1,0:T(8,128)(2,1)} %get-tuple-element.8.q, bf16[2,64,1024]{2,1,0:T(8,128)(2,1)} %get-tuple-element.9.k, bf16[2,64,1024]{2,1,0:T(8,128)(2,1)} %get-tuple-element.10.v, ...), custom_call_target="tpu_custom_call" | custom-call | tf_op jit(solution)/shard_map/pallas_call | solution.py:441

commit v4 on v3

--- a/solution.py
+++ b/solution.py
@@ -70,7 +70,7 @@
     factor = D ** (-0.5)
     level = me // quarter
     ring = me % quarter
-    near = ((level + 1) // 2) % 2
+    near = 1 - level % 2
     low = level < 2
     slots = 1 + (SLOTS - 1) * near
 
@@ -156,7 +156,7 @@
         def send(step, carry):
             spot = spot_of(step, side)
             pair = group * quarter + spot
-            low_home = (1 - far) * quarter + spot
+            low_home = far * quarter + spot
             high_home = half + far * quarter + spot
 
             def source(number):

time: 72.3 us -> 70.4 us (0.974)
  Pallas kernels: 71.5 us -> 69.6 us
    pallas_call x1, Pallas kernels: 68.3 us -> 66.4 us  [local(): pl.pallas_call(functools.partial(kernel, n, m, local_heads), out_shape=(r...]
where the time goes in v4:
time: 70.4 us; the launch traced here: 70.2 us
  Pallas kernels  69.6 us (99%)
    pallas_call x1, Pallas kernels, local(): pl.pallas_call(functools.partial(kernel, n, m, local_heads), out_shape=(r...  66.4 us
    pallas_call x1, Pallas kernels, local(): pl.pallas_call(hand_over, out_shape=(result, result, result, jax.ShapeDty...  3.19 us

profile of v4, /device:TPU:0, one launch (start us, length us, event | category | flops | bytes accessed | tf_op | source)
XLA Modules:
  0.0 70.2 jit_solution(10613984713405128882)
XLA Ops:
  0.6 66.4 %shard_map.93 = (bf16[2,64,1024]{2,1,0:T(8,128)(2,1)}, bf16[2,64,1024]{2,1,0:T(8,128)(2,1)}, bf16[2,64,1024]{2,1,0:T(8,128)(2,1)}, f32[2,16]{1,0:T(2,128)}) custom-call(bf16[2,64,1024]{2,1,0:T(8,128)(2,1)} %q_in.1, bf16[2,64,1024]{2,1,0:T(8,128)(2,1)} %k_in.1, bf16[2,64,1024]{2,1,0:T(8,128)(2,1)} %v_in.1, bf16[2,64,1024]{2,1,0:T(8,128)(2,1)} %tq_in.1, ...), custom_call_target="tpu_custom_call" | custom-call | tf_op jit(solution)/shard_map/pallas_call | solution.py:408
  67.0 3.2 %shard_map.94 = (bf16[2,64,1024]{2,1,0:T(8,128)(2,1)}, bf16[2,64,1024]{2,1,0:T(8,128)(2,1)}, bf16[2,64,1024]{2,1,0:T(8,128)(2,1)}, f32[2,16]{1,0:T(2,128)}) custom-call(bf16[2,64,1024]{2,1,0:T(8,128)(2,1)} %get-tuple-element.8.q, bf16[2,64,1024]{2,1,0:T(8,128)(2,1)} %get-tuple-element.9.k, bf16[2,64,1024]{2,1,0:T(8,128)(2,1)} %get-tuple-element.10.v, ...), custom_call_target="tpu_custom_call" | custom-call | tf_op jit(solution)/shard_map/pallas_call | solution.py:441

commit v5 on v2

--- a/solution.py
+++ b/solution.py
@@ -68,7 +68,7 @@
     factor = D ** (-0.5)
     level = me // quarter
     ring = me % quarter
-    near = ((level + 1) // 2) % 2
+    near = 1 - level % 2
     low = level < 2
     slots = 1 + (SLOTS - 1) * near
 
@@ -125,15 +125,15 @@
         def send(step, carry, group=group, far=far, slot=slot):
             spot = (me + step) % quarter
             pair = group * quarter + spot
-            low_home = (1 - far) * quarter + spot
+            low_home = far * quarter + spot
             high_home = half + far * quarter + spot
 
             @pl.when(low)
             def _():
+                for number in range(6):
+                    feed(number, pair, slot, low_home, me * tokens)
                 for number in range(3):
                     feed(number, pair, slot, high_home, me * tokens)
-                for number in range(6):
-                    feed(number, pair, slot, low_home, me * tokens)
 
             @pl.when(jnp.logical_not(low))
             def _():

time: 70.8 us -> 67.8 us (0.958)
  Pallas kernels: 66 us -> 63 us
    pallas_call x1, Pallas kernels: 66 us -> 63 us  [local(): pl.pallas_call(functools.partial(kernel, n, m, local_heads), out_shape=(r...]
where the time goes in v5:
time: 67.8 us; the launch traced here: 67.6 us
  Pallas kernels  63 us (93%)
  local copies, waits for them, and re-layouts  4.03 us (6%)
    pallas_call x1, Pallas kernels, local(): pl.pallas_call(functools.partial(kernel, n, m, local_heads), out_shape=(r...  63 us
    unnamed x10, local copies, waits for them, and re-layouts  4.03 us

profile of v5, /device:TPU:0, one launch (start us, length us, event | category | flops | bytes accessed | tf_op | source)
XLA Modules:
  0.0 67.6 jit_solution(1802469988388234576)
XLA Ops:
  0.6 63.0 %shard_map.93 = (bf16[2,64,1024]{2,1,0:T(8,128)(2,1)}, bf16[2,64,1024]{2,1,0:T(8,128)(2,1)}, bf16[2,64,1024]{2,1,0:T(8,128)(2,1)}, f32[2,16]{1,0:T(2,128)}) custom-call(bf16[2,64,1024]{2,1,0:T(8,128)(2,1)} %q_in.1, bf16[2,64,1024]{2,1,0:T(8,128)(2,1)} %k_in.1, bf16[2,64,1024]{2,1,0:T(8,128)(2,1)} %v_in.1, bf16[2,64,1024]{2,1,0:T(8,128)(2,1)} %tq_in.1, ...), custom_call_target="tpu_custom_call" | custom-call | tf_op jit(solution)/shard_map/pallas_call | solution.py:339
  63.6 0.0 copy-start.1
  63.6 1.7 %copy.14 = bf16[2,64,1024]{2,1,0:T(8,128)(2,1)} copy(bf16[2,64,1024]{2,1,0:T(8,128)(2,1)} %get-tuple-element.8) | data formatting | bytes 524288
  65.3 0.0 copy-done.1
  65.3 0.0 copy-start
  65.3 0.7 %copy.15 = bf16[2,64,1024]{2,1,0:T(8,128)(2,1)} copy(bf16[2,64,1024]{2,1,0:T(8,128)(2,1)S(1)} %copy-done.1) | data formatting | bytes 524288
  66.0 0.3 copy-done
  66.4 0.0 copy-start.2
  66.4 0.7 %copy.16 = bf16[2,64,1024]{2,1,0:T(8,128)(2,1)} copy(bf16[2,64,1024]{2,1,0:T(8,128)(2,1)S(1)} %copy-done) | data formatting | bytes 524288
  67.1 0.0 copy-done.2
  67.1 0.6 copy.17
Async XLA Ops:
  63.6 1.7 %copy-start.1 = (bf16[2,64,1024]{2,1,0:T(8,128)(2,1)S(1)}, bf16[2,64,1024]{2,1,0:T(8,128)(2,1)}, u32[]{:S(2)}) copy-start(bf16[2,64,1024]{2,1,0:T(8,128)(2,1)} %get-tuple-element.9) | copy-start | bytes 786436
  65.3 1.0 %copy-start = (bf16[2,64,1024]{2,1,0:T(8,128)(2,1)S(1)}, bf16[2,64,1024]{2,1,0:T(8,128)(2,1)}, u32[]{:S(2)}) copy-start(bf16[2,64,1024]{2,1,0:T(8,128)(2,1)} %get-tuple-element.10) | copy-start | bytes 786436
  66.4 0.7 %copy-start.2 = (f32[2,16]{1,0:T(2,128)S(1)}, f32[2,16]{1,0:T(2,128)}, u32[]{:S(2)}) copy-start(f32[2,16]{1,0:T(2,128)} %get-tuple-element.11) | copy-start | bytes 388
